TPU v7x, 256 devices: a whole 4x4x8 slice. The times are simulated.
256 devices in a mesh: seq: 32 (over y, z), tensor: 8 (over x, core).
Axes of the slice: x: 4, y: 4, z: 8, core: 2. Of those that a mesh axis runs over, the one named last changes fastest.
Arguments:
- state: bfloat16 [32768, 2048], P('seq', 'tensor'), may hold values from -20.5 to 20.5
- memory: bfloat16 [512, 2048], P('seq', 'tensor'), may hold values from -20.5 to 20.5
- w_query: bfloat16 [2048, 2048], P('seq', 'tensor'), may hold values from -0.1875 to 0.1875
- w_key: bfloat16 [2048, 2048], P('seq', 'tensor'), may hold values from -0.1875 to 0.1875
- w_value: bfloat16 [2048, 2048], P('seq', 'tensor'), may hold values from -0.125 to 0.125
- w_output: bfloat16 [2048, 2048], P('tensor', 'seq'), may hold values from -0.375 to 0.375
- norm_gain: float32 [2048], P('tensor'), may hold values from 0.1 to 1.9
- remaining: int32 [32768], P('seq'), may hold values from 0 to 3
- slot_home: int32 [512], replicated, may hold values from 0 to 31
Outputs:
- new_state: bfloat16 [32768, 2048], P('seq', 'tensor')
- new_memory: bfloat16 [512, 2048], P('seq', 'tensor')
Inputs may be any that keep to these rules, and one draw needn't show every extreme that they name: `remaining`: 0 means the token has halted.
All inputs are finite; a program needn't handle non-finite values.
Results may differ from a plain program's by a relative error of at most 0.014.
The roundings to bfloat16 on the way count: a program that leaves them out, or rounds other values in their place, can miss the bound.
Values may be sent and summed in bfloat16 or wider, within the bound.
No kernel may reach another device: no remote copies, remote signals or barrier semaphores. Data moves between devices by JAX's collectives and lax.ppermute only.
A program may use at most 128 MiB of HBM per device.

v0:
```python
import math
import jax
import jax.numpy as jnp
from jax import lax
from jax.sharding import PartitionSpec as P

D = 2048
H = 16
HD = 128
HALF = 256
QB = 512
EPS = 1e-05
MASKED = -1e30


def with_halo(array, sides, width):
    for axis, dim in sides:
        peers, length = (lax.axis_size(axis), array.shape[dim])
        up = [(i, (i + 1) % peers) for i in range(peers - 1)]
        down = [(j, i) for i, j in up]
        last = lax.slice_in_dim(array, length - width, length, axis=dim)
        initial = lax.slice_in_dim(array, 0, width, axis=dim)
        before = lax.ppermute(last, axis, up)
        after = lax.ppermute(initial, axis, down)
        array = jnp.concatenate([before, array, after], axis=dim)
    return array


def merged(part, axis, combine):
    gathered = jax.tree.map(lambda a: lax.all_gather(a, axis), part)

    def take(source):
        return jax.tree.map(lambda a: lax.dynamic_index_in_dim(a, source, 0, False), gathered)

    return lax.fori_loop(
        1, lax.axis_size(axis), lambda source, state: combine(state, take(source)), take(0)
    )


def head_slopes(first, amount):
    order = (first + jnp.arange(amount, dtype=jnp.int32)).astype(jnp.float32)
    return 0.25 * 8.0 ** (order / (H - 1))


def shards(state, memory, w_query, w_key, w_value, w_output, norm_gain, remaining, slot_home):
    tok_rows = state.shape[0]
    slot_rows = memory.shape[0]
    seq_count = lax.axis_size("seq")
    seq_place = lax.axis_index("seq")
    tensor_place = lax.axis_index("tensor")
    local_width = w_query.shape[1]
    local_heads = local_width // HD
    total_tokens = tok_rows * seq_count
    score_scale = 1.0 / math.sqrt(HD)
    distance_slopes = head_slopes(tensor_place * local_heads, local_heads)
    homes = slot_home.astype(jnp.float32)
    home_gap = jnp.abs(homes - seq_place.astype(jnp.float32))
    slot_bias = distance_slopes[:, None] * home_gap[None, :]
    state_full, memory_full = (
        lax.all_gather(state, "tensor", axis=1, tiled=True),
        lax.all_gather(memory, "tensor", axis=1, tiled=True),
    )
    rows_full = jnp.concatenate([state_full, memory_full], axis=0)
    pieces = (
        lax.all_gather(w_query, "seq", axis=0, tiled=True),
        lax.all_gather(w_key, "seq", axis=0, tiled=True),
        lax.all_gather(w_value, "seq", axis=0, tiled=True),
    )
    query_acc, key_acc, value_acc = tuple(
        (jnp.dot(rows_full, piece, preferred_element_type=jnp.float32) for piece in pieces)
    )
    query = query_acc.astype(jnp.bfloat16)
    keys = key_acc.astype(jnp.bfloat16)
    values = value_acc.astype(jnp.bfloat16)
    slot_heads = jnp.concatenate([query[tok_rows:], keys[tok_rows:], values[tok_rows:]], axis=1)
    all_slots = lax.all_gather(slot_heads, "seq", axis=0, tiled=True)
    memory_slot_query = all_slots[:, :local_width].reshape(-1, local_heads, HD)
    memory_slot_keys = all_slots[:, local_width : 2 * local_width].reshape(-1, local_heads, HD)
    memory_slot_values = all_slots[:, 2 * local_width :].reshape(-1, local_heads, HD)
    token_key_rows = keys[:tok_rows].reshape(tok_rows, local_heads, HD)
    token_value_rows = values[:tok_rows].reshape(tok_rows, local_heads, HD)
    keys_values = jnp.concatenate([keys[:tok_rows], values[:tok_rows]], axis=1)
    padded = with_halo(keys_values, (("seq", 0),), HALF)
    block = QB
    window_extent = block + 2 * HALF

    def one_block(number):
        start = number * block
        query_matrix = lax.dynamic_slice_in_dim(query, start, block, 0).reshape(
            block, local_heads, HD
        )
        near_rows = lax.dynamic_slice_in_dim(padded, start, window_extent, 0)
        near_keys = near_rows[:, :local_width].reshape(window_extent, local_heads, HD)
        near_values = near_rows[:, local_width:].reshape(window_extent, local_heads, HD)
        near = (
            jnp.einsum("qhd,khd->hqk", query_matrix, near_keys, preferred_element_type=jnp.float32)
            * score_scale
        )
        first = seq_place * tok_rows + start
        qpos = first + jnp.arange(block, dtype=jnp.int32)
        kpos = first - HALF + jnp.arange(window_extent, dtype=jnp.int32)
        valid = (
            (jnp.abs(qpos[:, None] - kpos[None, :]) <= HALF)
            & (kpos >= 0)[None, :]
            & (kpos < total_tokens)[None, :]
        )
        near = jnp.where(valid[None], near, MASKED)
        distant_mask = (
            jnp.einsum(
                "taw,caw->atc", query_matrix, memory_slot_keys, preferred_element_type=jnp.float32
            )
            * score_scale
            - slot_bias[:, None, :]
        )
        scores = jnp.concatenate([near, distant_mask], axis=2)
        top = jnp.max(scores, axis=2, keepdims=True)
        exponent_terms = jnp.exp(scores - top)
        total = jnp.sum(exponent_terms, axis=2)
        attention_probabilities = exponent_terms.astype(jnp.bfloat16)
        numer = jnp.einsum(
            "hqk,khd->qhd",
            attention_probabilities[:, :, :window_extent],
            near_values,
            preferred_element_type=jnp.float32,
        )
        numer = numer + jnp.einsum(
            "lse,elf->slf",
            attention_probabilities[:, :, window_extent:],
            memory_slot_values,
            preferred_element_type=jnp.float32,
        )
        return (
            (numer / jnp.transpose(total)[:, :, None])
            .astype(jnp.bfloat16)
            .reshape(block, local_width)
        )

    token_mix = lax.map(one_block, jnp.arange(tok_rows // block, dtype=jnp.int32)).reshape(
        tok_rows, local_width
    )
    unnormalized_scores = (
        jnp.einsum(
            "gki,pki->kgp", memory_slot_query, token_key_rows, preferred_element_type=jnp.float32
        )
        * score_scale
        - slot_bias[:, :, None]
    )
    local_top = jnp.max(unnormalized_scores, axis=2)
    exponent_terms = jnp.exp(unnormalized_scores - local_top[:, :, None])
    local_sum = jnp.transpose(jnp.sum(exponent_terms, axis=2))
    local_num = jnp.einsum(
        "xzg,gxw->zxw",
        exponent_terms.astype(jnp.bfloat16),
        token_value_rows,
        preferred_element_type=jnp.float32,
    )
    local_top = jnp.transpose(local_top)

    def combine(first_part, second_part):
        top = jnp.maximum(first_part[0], second_part[0])
        weight_first = jnp.exp(first_part[0] - top)
        weight_second = jnp.exp(second_part[0] - top)
        sums = weight_first * first_part[1] + weight_second * second_part[1]
        numers = (
            weight_first[:, :, None] * first_part[2] + weight_second[:, :, None] * second_part[2]
        )
        return (top, sums, numers)

    merged_parts = merged((local_top, local_sum, local_num), "seq", combine)
    own_sum = lax.dynamic_slice_in_dim(merged_parts[1], seq_place * slot_rows, slot_rows, 0)
    own_num = lax.dynamic_slice_in_dim(merged_parts[2], seq_place * slot_rows, slot_rows, 0)
    slot_mix = (own_num / own_sum[:, :, None]).astype(jnp.bfloat16).reshape(slot_rows, local_width)
    mixed = jnp.concatenate([token_mix, slot_mix], axis=0)
    partial_rows = jnp.dot(
        mixed,
        lax.all_gather(w_output, "seq", axis=1, tiled=True),
        preferred_element_type=jnp.float32,
    )
    summed = lax.psum_scatter(
        partial_rows.astype(jnp.bfloat16), "tensor", scatter_dimension=1, tiled=True
    ).astype(jnp.float32)
    residual = jnp.concatenate([state, memory], axis=0).astype(jnp.float32) + summed
    squares = lax.psum(jnp.sum(residual * residual, axis=1), "tensor")
    normed_rows = (residual * lax.rsqrt(squares / D + EPS)[:, None] * norm_gain[None, :]).astype(
        jnp.bfloat16
    )
    new_state = jnp.where((remaining > 0)[:, None], normed_rows[:tok_rows], state)
    new_memory = normed_rows[tok_rows:]
    return (new_state, new_memory)


def solution(mesh):
    placed = (
        P("seq", "tensor"),
        P("seq", "tensor"),
        P("seq", "tensor"),
        P("seq", "tensor"),
        P("seq", "tensor"),
        P("tensor", "seq"),
        P("tensor"),
        P("seq"),
        P(),
    )
    return jax.shard_map(
        shards,
        mesh=mesh,
        in_specs=placed,
        out_specs=(P("seq", "tensor"), P("seq", "tensor")),
        check_vma=False,
    )
```

profile of v0, /device:TPU:1, one launch (start us, length us, event | category | flops | bytes accessed | tf_op | source)
XLA Modules:
  0.0 714.2 jit_solution(8940133622111685820)
XLA Ops:
  10.7 16.0 %all_gather.40 = bf16[16,2048]{1,0:T(8,128)(2,1)S(1)} all-gather(bf16[16,256]{1,0:T(8,128)(2,1)} %param.14), channel_id=1, replica_groups=mesh['seq'=32,'tensor'=8] {'tensor'}, dimensions={1}, use_global_device_ids=true | all-gather | bytes 73728 | tf_op jit(solution)/shard_map/all_gather | solution.py:61
  26.8 25.3 %all-gather.10.cloned.1.call-done = bf16[1024,2048]{1,0:T(8,128)(2,1)} async-done(((bf16[1024,256]{1,0:T(8,128)(2,1)}), bf16[1024,2048]{1,0:T(8,128)(2,1)}) %all-gather.10.cloned.1.call-update) | async-done | bytes 4194320 | tf_op jit(solution)/shard_map/all_gather | solution.py:60
  52.1 4.7 constant_dynamic-update-slice_fusion.2
  57.4 69.1 %all-gather.14.cloned.1.call-done = bf16[2048,256]{1,0:T(8,128)(2,1)} async-done(((bf16[64,256]{1,0:T(8,128)(2,1)}), bf16[2048,256]{1,0:T(8,128)(2,1)}) %all-gather.14.cloned.1.call-update) | async-done | bytes 1048592 | tf_op jit(solution)/shard_map/all_gather | solution.py:67
  126.5 3.8 convolution_convert_fusion.2
  130.4 72.6 %all-gather.12.cloned.1.call-done = bf16[2048,256]{1,0:T(8,128)(2,1)} async-done(((bf16[64,256]{1,0:T(8,128)(2,1)}), bf16[2048,256]{1,0:T(8,128)(2,1)}) %all-gather.12.cloned.1.call-update) | async-done | bytes 1048592 | tf_op jit(solution)/shard_map/all_gather | solution.py:66
  203.0 3.8 convolution_convert_fusion.3
  206.9 72.4 %all-gather.16.cloned.1.call-done = bf16[2048,256]{1,0:T(8,128)(2,1)} async-done(((bf16[64,256]{1,0:T(8,128)(2,1)}), bf16[2048,256]{1,0:T(8,128)(2,1)}) %all-gather.16.cloned.1.call-update) | async-done | bytes 1048592 | tf_op jit(solution)/shard_map/all_gather | solution.py:65
  279.3 3.8 convolution_convert_fusion.1
  284.1 36.9 %all_gather.44 = bf16[512,768]{1,0:T(8,128)(2,1)S(1)} all-gather(bf16[16,768]{1,0:T(8,128)(2,1)S(1)} %pad_maximum_fusion.4), channel_id=1, replica_groups=mesh['seq'=32,'tensor'=8] {'seq'}, dimensions={0}, use_global_device_ids=true | all-gather | bytes 811008 | tf_op jit(solution)/shard_map/all_gather | solution.py:76
  332.0 36.6 %all-gather = f32[16384,2]{0,1:T(2,128)S(1)} all-gather(f32[512,2]{0,1:T(2,128)S(1)} %bitcast.123), channel_id=2, replica_groups=mesh['seq'=32,'tensor'=8] {'seq'}, dimensions={0}, use_global_device_ids=true | all-gather | bytes 135168 | tf_op jit(solution)/shard_map/all_gather | solution.py:30
  371.9 35.7 %all-gather.1 = f32[16384,2]{0,1:T(2,128)S(1)} all-gather(f32[512,2]{0,1:T(2,128)S(1)} %bitcast.126), channel_id=3, replica_groups=mesh['seq'=32,'tensor'=8] {'seq'}, dimensions={0}, use_global_device_ids=true | all-gather | bytes 135168 | tf_op jit(solution)/shard_map/all_gather | solution.py:30
  409.9 22.6 %while.33 = (s32[]{:T(128)}, bf16[2,512,256]{2,1,0:T(8,128)(2,1)}, s32[2]{0:T(128)}, bf16[1536,512]{1,0:T(8,128)(2,1)S(1)}, s32[]{:T(128)}, /*index=5*/bf16[1040...) while((s32[]{:T(128)}, bf16[2,512,256]{2,1,0:T(8,128)(2,1)}, ...), condition=%wide.region_4.5_spmd.clone, body=%wide.region_0.4_spmd.clone.sunk | while | flops 819334656 | bytes 41282024 | solution.py:138
  432.4 48.4 %all-gather.20.cloned.1.call-done = f32[16384,2,128]{0,2,1:T(8,128)} async-done(((f32[512,2,128]{0,2,1:T(8,128)}), f32[16384,2,128]{0,2,1:T(8,128)}) %all-gather.20.cloned.1.call-update) | async-done | bytes 16777232 | tf_op jit(solution)/shard_map/all_gather | solution.py:30
  482.2 25.0 %copy.46 = f32[16384,2,128]{2,1,0:T(2,128)} copy(f32[16384,2,128]{0,2,1:T(8,128)} %all-gather.20.cloned.1.call-done) | data formatting | bytes 33554432 | tf_op jit(solution)/shard_map/while | solution.py:35
  507.1 140.4 %while.32 = (s32[]{:T(128)}, f32[512,2]{0,1:T(2,128)S(1)}, f32[512,2]{0,1:T(2,128)S(1)}, f32[512,2,128]{2,1,0:T(2,128)S(1)}, f32[32,512,2]{1,2,0:T(2,128)S(1)}, ...) while((s32[]{:T(128)}, f32[512,2]{0,1:T(2,128)S(1)}, ...), condition=%wide.region_8.9_spmd, body=%wide.region_7.8_spmd.sunk | while | flops 399365 | bytes 1630351 | solution.py:35
  508.2 3.5 fusion.77
  512.7 3.5 fusion.77
  517.3 3.5 fusion.77
  521.8 3.5 fusion.77
  526.3 3.5 fusion.77
  530.9 3.5 fusion.77
  535.4 3.5 fusion.77
  539.9 3.5 fusion.77
  544.5 3.5 fusion.77
  549.0 3.5 fusion.77
  553.5 3.5 fusion.77
  558.0 3.5 fusion.77
  562.5 3.5 fusion.77
  567.1 3.5 fusion.77
  571.6 3.5 fusion.77
  576.1 3.5 fusion.77
  580.7 3.5 fusion.77
  585.2 3.5 fusion.77
  589.7 3.5 fusion.77
  594.3 3.5 fusion.77
  598.8 3.5 fusion.77
  603.3 3.5 fusion.77
  607.8 3.5 fusion.77
  612.4 3.5 fusion.77
  616.9 3.5 fusion.77
  621.4 3.5 fusion.77
  626.0 3.5 fusion.77
  630.5 3.5 fusion.77
  635.0 3.5 fusion.77
  647.9 4.5 convolution_convert_fusion
  653.1 34.7 %reduce-scatter.2.cloned.1.call-done = bf16[1040,256]{1,0:T(8,128)(2,1)} async-done(((bf16[1040,2048]{1,0:T(8,128)(2,1)}), bf16[1040,256]{1,0:T(8,128)(2,1)}) %reduce-scatter.2.cloned.1.call-update) | async-done | bytes 532496 | tf_op jit(solution)/shard_map/reduce_scatter | solution.py:179
  689.1 15.3 %psum.7 = f32[1040]{0:T(1024)S(1)} all-reduce(f32[1040]{0:T(1024)S(1)} %multiply_reduce_fusion), channel_id=1, replica_groups=mesh['seq'=32,'tensor'=8] {'tensor'}, use_global_device_ids=true, to_apply=%region_11.12 | all-reduce | flops 1040 | bytes 8320 | tf_op jit(solution)/shard_map/psum | solution.py:183
  (233 shorter events, 87.3 us)
Async XLA Ops:
  7.2 44.9 %all-gather.10.cloned.1.call-start = ((), (), s32[]{:S(2)}) async-start(), calls=%async_computation.1 | async-start | bytes 4718592 | tf_op jit(solution)/shard_map/all_gather | solution.py:60
  7.9 118.6 %all-gather.14.cloned.1.call-start = ((), (), s32[]{:S(2)}) async-start(), calls=%async_computation.3 | async-start | bytes 1081344 | tf_op jit(solution)/shard_map/all_gather | solution.py:67
  8.6 194.4 %all-gather.12.cloned.1.call-start = ((), (), s32[]{:S(2)}) async-start(), calls=%async_computation.2 | async-start | bytes 1081344 | tf_op jit(solution)/shard_map/all_gather | solution.py:66
  9.4 270.0 %all-gather.16.cloned.1.call-start = ((), (), s32[]{:S(2)}) async-start(), calls=%async_computation.4 | async-start | bytes 1081344 | tf_op jit(solution)/shard_map/all_gather | solution.py:65
  10.0 470.9 %all-gather.20.cloned.1.call-start = ((), (), s32[]{:S(2)}) async-start(), calls=%async_computation.7 | async-start | bytes 17301504 | tf_op jit(solution)/shard_map/all_gather | solution.py:30
  10.7 46.1 %copy-start.11 = (f32[512]{0:T(512)}, f32[512]{0:T(512)S(1)}, u32[]{:S(2)}) copy-start(f32[512]{0:T(512)S(1)} %subtract_abs_fusion) | copy-start | bytes 6148
  26.7 30.1 %copy-start.14 = (f32[2]{0:T(128)}, f32[2]{0:T(128)S(1)}, u32[]{:S(2)}) copy-start(f32[2]{0:T(128)S(1)} %power_multiply_fusion) | copy-start | bytes 28
  26.8 295.1 %copy-start.13 = (f32[2,512]{1,0:T(2,128)}, f32[2,512]{1,0:T(2,128)S(1)}, u32[]{:S(2)}) copy-start(f32[2,512]{1,0:T(2,128)S(1)} %broadcast_multiply_fusion.1) | copy-start | bytes 12292
  284.1 39.7 %copy-start.8 = (bf16[1024,256]{0,1:T(8,128)(2,1)S(1)}, bf16[1024,256]{0,1:T(8,128)(2,1)}, u32[]{:S(2)}) copy-start(bf16[1024,256]{0,1:T(8,128)(2,1)} %copy.45) | copy-start | bytes 1572868
  321.9 1.9 copy-start
  325.9 322.0 %all-gather.18.cloned.1.call-start = ((), (), s32[]{:S(2)}) async-start(), calls=%async_computation.5 | async-start | bytes 1081344 | tf_op jit(solution)/shard_map/all_gather | solution.py:176
  326.5 361.3 %reduce-scatter.2.cloned.1.call-start = ((), (), s32[]{:S(2)}) async-start(), calls=%async_computation.6 | async-start | bytes 4792320 | tf_op jit(solution)/shard_map/reduce_scatter | solution.py:179
  326.6 81.1 %collective-permute-start = (bf16[256,512]{1,0:T(8,128)(2,1)S(1)}, bf16[256,512]{1,0:T(8,128)(2,1)S(1)}, u32[]{:S(2)}, u32[]{:S(2)}) collective-permute-start(bf16[256,512]{1,0:T(8,128)(2,1)S(1)} %get-tuple-element.403), channel_id=1, source_target_pairs={{0,8},{8,16},{16,24},{24,32},{32,40},{40,48},{48,56},{56,64},{64,7... | collective-permute-start | bytes 786440 | tf_op jit(solution)/shard_map/ppermute | solution.py:23
  329.1 79.2 %collective-permute-start.1 = (bf16[256,512]{1,0:T(8,128)(2,1)S(1)}, bf16[256,512]{1,0:T(8,128)(2,1)}, u32[]{:S(2)}, u32[]{:S(2)}) collective-permute-start(bf16[256,512]{1,0:T(8,128)(2,1)S(1)} %get-tuple-element.404), channel_id=1, source_target_pairs={{8,0},{16,8},{24,16},{32,24},{40,32},{48,40},{56,48},{64,56},{72,6... | collective-permute-start | bytes 786440 | tf_op jit(solution)/shard_map/ppermute | solution.py:24
  407.6 0.7 copy-start.10
  409.9 2.9 copy-start.3
  417.5 1.3 copy-start.1
  417.6 2.1 copy-start.9
  418.8 1.5 copy-start.5
  418.8 2.3 copy-start.4
  420.3 0.8 copy-start.6
  421.1 2.9 copy-start.3
  428.8 1.3 copy-start.1
  428.8 2.1 copy-start.9
  430.1 1.5 copy-start.5
  430.1 2.3 copy-start.4
  431.6 0.8 copy-start.6
  507.1 140.7 %copy-start.7 = (bf16[2,512,256]{2,1,0:T(8,128)(2,1)S(1)}, bf16[2,512,256]{2,1,0:T(8,128)(2,1)}, u32[]{:S(2)}) copy-start(bf16[2,512,256]{2,1,0:T(8,128)(2,1)} %get-tuple-element.294) | copy-start | bytes 1572868
  652.4 0.7 copy-start.15
  652.4 35.4 %copy-start.2 = (bf16[1024,256]{1,0:T(8,128)(2,1)S(1)}, bf16[1024,256]{1,0:T(8,128)(2,1)}, u32[]{:S(2)}) copy-start(bf16[1024,256]{1,0:T(8,128)(2,1)} %param.13) | copy-start | bytes 1572868
  652.4 35.4 %copy-start.12 = (bf16[16,256]{1,0:T(8,128)(2,1)S(1)}, bf16[16,256]{1,0:T(8,128)(2,1)}, u32[]{:S(2)}) copy-start(bf16[16,256]{1,0:T(8,128)(2,1)} %param.14) | copy-start | bytes 24580
  652.4 52.0 %copy-start.16 = (f32[256]{0:T(256)S(1)}, f32[256]{0:T(256)}, u32[]{:S(2)}) copy-start(f32[256]{0:T(256)} %param.19) | copy-start | bytes 3076
Sparse Core Ops, SparseCore 0:
  9.8 42.2 all-gather.9
  54.7 71.8 all-gather.13
  129.1 73.8 all-gather.11
  205.5 73.8 all-gather.15
  326.0 154.7 all-gather.19
  483.3 68.5 all-gather.17
  652.5 35.1 reduce-scatter.1
where the time goes:
time: 718 us; the launch traced here: 714 us
  waiting for transfers between devices  326 us (45%)
  other arithmetic  144 us (20%)
  blocking collectives  141 us (20%)
  local copies, waits for them, and re-layouts  55.6 us (8%)
  matrix products  26.7 us (4%)
  between operations  14.4 us (2%)
    add x31, other arithmetic, combine(): weight_first[:, :, None] * first_part[2]  108 us
    all_gather x1, waiting for transfers between devices, shards(): lax.all_gather(w_key, 'seq', axis=0, tiled=True)  72.6 us
    all_gather x1, waiting for transfers between devices, shards(): lax.all_gather(w_query, 'seq', axis=0, tiled=True)  72.4 us
    all_gather x2, blocking collectives, merged(): gathered = jax.tree.map(lambda a: lax.all_gather(a, axis), part)  72.3 us
    all_gather x1, waiting for transfers between devices, shards(): lax.all_gather(w_value, 'seq', axis=0, tiled=True)  69.1 us
    all_gather x1, waiting for transfers between devices, merged(): gathered = jax.tree.map(lambda a: lax.all_gather(a, axis), part)  48.4 us
    all_gather x1, blocking collectives, shards(): all_slots = lax.all_gather(slot_heads, 'seq', axis=0, tiled=True)  36.9 us
    reduce_scatter x1, waiting for transfers between devices, shards(): lax.psum_scatter(partial_rows.astype(jnp.bfloat16), 'tensor', scatter_dim...  34.7 us
  transfers between devices with their start and end apart: 9, of which 6 were waited for; matrix products, arithmetic and copies ran while one was open for 29% of the time, Pallas kernels for 0%

commit v1 on v0

--- a/solution.py
+++ b/solution.py
@@ -61,10 +61,18 @@
         lax.all_gather(memory, "tensor", axis=1, tiled=True),
     )
     rows_full = jnp.concatenate([state_full, memory_full], axis=0)
+
+    def remake_classes(field):
+        e_next = tuple((field for _ in range(lax.axis_size("seq"))))
+        r2 = jnp.stack(e_next, axis=0)
+        t1 = lax.all_to_all(r2, "seq", split_axis=0, concat_axis=0)
+        high = jnp.concatenate(t1, 0)
+        return high
+
     pieces = (
         lax.all_gather(w_query, "seq", axis=0, tiled=True),
         lax.all_gather(w_key, "seq", axis=0, tiled=True),
-        lax.all_gather(w_value, "seq", axis=0, tiled=True),
+        remake_classes(w_value),
     )
     query_acc, key_acc, value_acc = tuple(
         (jnp.dot(rows_full, piece, preferred_element_type=jnp.float32) for piece in pieces)

time: 718 us -> 642 us (0.89)
  waiting for transfers between devices: 326 us -> 238 us
  starting transfers between devices: 4.04 us -> 16 us
    all_gather x1 -> x0, waiting for transfers between devices: 69.1 us -> none  [shards(): lax.all_gather(w_value, 'seq', axis=0, tiled=True)]
    all_to_all x0 -> x1, starting transfers between devices: none -> 12 us  [remake_classes(): t1 = lax.all_to_all(r2, 'seq', split_axis=0, concat_axis=0)]
    all_gather x1, waiting for transfers between devices: 25.3 us -> 13.9 us  [shards(): lax.all_gather(state, 'tensor', axis=1, tiled=True)]
  transfers between devices with their start and end apart: 9 -> 9, of which waited for: 6 -> 5; matrix products, arithmetic and copies ran while one was open for 29% -> 32% of each run, Pallas kernels for 0% -> 0%
where the time goes in v1:
time: 642 us; the launch traced here: 638 us
  waiting for transfers between devices  238 us (37%)
  other arithmetic  144 us (22%)
  blocking collectives  139 us (22%)
  local copies, waits for them, and re-layouts  57.6 us (9%)
  matrix products  26.4 us (4%)
  starting transfers between devices  16 us (2%)
  between operations  14.4 us (2%)
    add x31, other arithmetic, combine(): weight_first[:, :, None] * first_part[2]  108 us
    all_gather x1, waiting for transfers between devices, shards(): lax.all_gather(w_query, 'seq', axis=0, tiled=True)  72.5 us
    all_gather x2, blocking collectives, merged(): gathered = jax.tree.map(lambda a: lax.all_gather(a, axis), part)  72.4 us
    all_gather x1, waiting for transfers between devices, shards(): lax.all_gather(w_key, 'seq', axis=0, tiled=True)  65.6 us
    all_gather x1, waiting for transfers between devices, merged(): gathered = jax.tree.map(lambda a: lax.all_gather(a, axis), part)  48.2 us
    all_gather x1, blocking collectives, shards(): all_slots = lax.all_gather(slot_heads, 'seq', axis=0, tiled=True)  36.9 us
    reduce_scatter x1, waiting for transfers between devices, shards(): lax.psum_scatter(partial_rows.astype(jnp.bfloat16), 'tensor', scatter_dim...  34.6 us
    while x2, local copies, waits for them, and re-layouts, merged(): lax.fori_loop(1, lax.axis_size(axis), lambda source, state: combine(state...  25.2 us
  transfers between devices with their start and end apart: 9, of which 5 were waited for; matrix products, arithmetic and copies ran while one was open for 32% of the time, Pallas kernels for 0%

profile of v1, /device:TPU:1, one launch (start us, length us, event | category | flops | bytes accessed | tf_op | source)
XLA Modules:
  0.0 637.9 jit_solution(959577427608948657)
XLA Ops:
  10.5 12.0 %all-to-all-start = ((bf16[32,64,256]{2,1,0:T(8,128)(2,1)}), bf16[32,64,256]{2,1,0:T(8,128)(2,1)S(1)}, u32[]{:S(2)}, u32[]{:S(2)}) async-start(bf16[32,64,256]{2,1,0:T(8,128)(2,1)} %stack.2), calls=%async_computation | async-start | bytes 2097152 | tf_op jit(solution)/shard_map/all_to_all | solution.py:68
  24.0 14.2 %all_gather.37 = bf16[16,2048]{1,0:T(8,128)(2,1)S(1)} all-gather(bf16[16,256]{1,0:T(8,128)(2,1)} %param.14), channel_id=1, replica_groups=mesh['seq'=32,'tensor'=8] {'tensor'}, dimensions={1}, use_global_device_ids=true | all-gather | bytes 73728 | tf_op jit(solution)/shard_map/all_gather | solution.py:61
  38.3 13.9 %all-gather.9.cloned.1.call-done = bf16[1024,2048]{1,0:T(8,128)(2,1)} async-done(((bf16[1024,256]{1,0:T(8,128)(2,1)}), bf16[1024,2048]{1,0:T(8,128)(2,1)}) %all-gather.9.cloned.1.call-update) | async-done | bytes 4194320 | tf_op jit(solution)/shard_map/all_gather | solution.py:60
  52.3 4.7 constant_dynamic-update-slice_fusion.2
  61.2 65.6 %all-gather.11.cloned.1.call-done = bf16[2048,256]{1,0:T(8,128)(2,1)} async-done(((bf16[64,256]{1,0:T(8,128)(2,1)}), bf16[2048,256]{1,0:T(8,128)(2,1)}) %all-gather.11.cloned.1.call-update) | async-done | bytes 1048592 | tf_op jit(solution)/shard_map/all_gather | solution.py:74
  126.7 3.8 convolution_convert_fusion.3
  130.6 72.5 %all-gather.13.cloned.1.call-done = bf16[2048,256]{1,0:T(8,128)(2,1)} async-done(((bf16[64,256]{1,0:T(8,128)(2,1)}), bf16[2048,256]{1,0:T(8,128)(2,1)}) %all-gather.13.cloned.1.call-update) | async-done | bytes 1048592 | tf_op jit(solution)/shard_map/all_gather | solution.py:73
  203.2 3.8 convolution_convert_fusion.1
  208.0 36.9 %all_gather.40 = bf16[512,768]{1,0:T(8,128)(2,1)S(1)} all-gather(bf16[16,768]{1,0:T(8,128)(2,1)S(1)} %pad_maximum_fusion.4), channel_id=1, replica_groups=mesh['seq'=32,'tensor'=8] {'seq'}, dimensions={0}, use_global_device_ids=true | all-gather | bytes 811008 | tf_op jit(solution)/shard_map/all_gather | solution.py:84
  255.8 36.7 %all-gather = f32[16384,2]{0,1:T(2,128)S(1)} all-gather(f32[512,2]{0,1:T(2,128)S(1)} %bitcast.125), channel_id=2, replica_groups=mesh['seq'=32,'tensor'=8] {'seq'}, dimensions={0}, use_global_device_ids=true | all-gather | bytes 135168 | tf_op jit(solution)/shard_map/all_gather | solution.py:30
  295.8 35.7 %all-gather.1 = f32[16384,2]{0,1:T(2,128)S(1)} all-gather(f32[512,2]{0,1:T(2,128)S(1)} %bitcast.128), channel_id=3, replica_groups=mesh['seq'=32,'tensor'=8] {'seq'}, dimensions={0}, use_global_device_ids=true | all-gather | bytes 135168 | tf_op jit(solution)/shard_map/all_gather | solution.py:30
  333.7 22.7 %while.33 = (s32[]{:T(128)}, bf16[2,512,256]{2,1,0:T(8,128)(2,1)}, s32[2]{0:T(128)}, bf16[1536,512]{1,0:T(8,128)(2,1)S(1)}, s32[]{:T(128)}, /*index=5*/bf16[1040...) while((s32[]{:T(128)}, bf16[2,512,256]{2,1,0:T(8,128)(2,1)}, ...), condition=%wide.region_4.5_spmd.clone, body=%wide.region_0.4_spmd.clone.sunk | while | flops 819334656 | bytes 41282024 | solution.py:146
  356.4 48.2 %all-gather.17.cloned.1.call-done = f32[16384,2,128]{0,2,1:T(8,128)} async-done(((f32[512,2,128]{0,2,1:T(8,128)}), f32[16384,2,128]{0,2,1:T(8,128)}) %all-gather.17.cloned.1.call-update) | async-done | bytes 16777232 | tf_op jit(solution)/shard_map/all_gather | solution.py:30
  406.0 25.0 %copy.46 = f32[16384,2,128]{2,1,0:T(2,128)} copy(f32[16384,2,128]{0,2,1:T(8,128)} %all-gather.17.cloned.1.call-done) | data formatting | bytes 33554432 | tf_op jit(solution)/shard_map/while | solution.py:35
  430.9 140.4 %while.32 = (s32[]{:T(128)}, f32[512,2]{0,1:T(2,128)S(1)}, f32[512,2]{0,1:T(2,128)S(1)}, f32[512,2,128]{2,1,0:T(2,128)S(1)}, f32[32,512,2]{1,2,0:T(2,128)S(1)}, ...) while((s32[]{:T(128)}, f32[512,2]{0,1:T(2,128)S(1)}, ...), condition=%wide.region_8.9_spmd, body=%wide.region_7.8_spmd.sunk | while | flops 399365 | bytes 1630351 | solution.py:35
  432.0 3.5 fusion.77
  436.5 3.5 fusion.77
  441.1 3.5 fusion.77
  445.6 3.5 fusion.77
  450.1 3.5 fusion.77
  454.6 3.5 fusion.77
  459.2 3.5 fusion.77
  463.7 3.5 fusion.77
  468.2 3.5 fusion.77
  472.8 3.5 fusion.77
  477.3 3.5 fusion.77
  481.8 3.5 fusion.77
  486.4 3.5 fusion.77
  490.9 3.5 fusion.77
  495.4 3.5 fusion.77
  499.9 3.5 fusion.77
  504.5 3.5 fusion.77
  509.0 3.5 fusion.77
  513.5 3.5 fusion.77
  518.1 3.5 fusion.77
  522.6 3.5 fusion.77
  527.1 3.5 fusion.77
  531.6 3.5 fusion.77
  536.2 3.5 fusion.77
  540.7 3.5 fusion.77
  545.2 3.5 fusion.77
  549.7 3.5 fusion.77
  554.3 3.5 fusion.77
  558.8 3.5 fusion.77
  563.3 3.5 fusion.77
  571.7 4.5 convolution_convert_fusion
  576.9 34.6 %reduce-scatter.2.cloned.1.call-done = bf16[1040,256]{1,0:T(8,128)(2,1)} async-done(((bf16[1040,2048]{1,0:T(8,128)(2,1)}), bf16[1040,256]{1,0:T(8,128)(2,1)}) %reduce-scatter.2.cloned.1.call-update) | async-done | bytes 532496 | tf_op jit(solution)/shard_map/reduce_scatter | solution.py:187
  612.8 15.4 %psum.7 = f32[1040]{0:T(1024)S(1)} all-reduce(f32[1040]{0:T(1024)S(1)} %multiply_reduce_fusion), channel_id=1, replica_groups=mesh['seq'=32,'tensor'=8] {'tensor'}, use_global_device_ids=true, to_apply=%region_11.12 | all-reduce | flops 1040 | bytes 8320 | tf_op jit(solution)/shard_map/psum | solution.py:191
  (233 shorter events, 88.7 us)
Async XLA Ops:
  7.2 45.1 %all-gather.9.cloned.1.call-start = ((), (), s32[]{:S(2)}) async-start(), calls=%async_computation.2 | async-start | bytes 4718592 | tf_op jit(solution)/shard_map/all_gather | solution.py:60
  7.9 118.8 %all-gather.11.cloned.1.call-start = ((), (), s32[]{:S(2)}) async-start(), calls=%async_computation.3 | async-start | bytes 1081344 | tf_op jit(solution)/shard_map/all_gather | solution.py:74
  10.5 47.1 %all-to-all-start = ((bf16[32,64,256]{2,1,0:T(8,128)(2,1)}), bf16[32,64,256]{2,1,0:T(8,128)(2,1)S(1)}, u32[]{:S(2)}, u32[]{:S(2)}) async-start(bf16[32,64,256]{2,1,0:T(8,128)(2,1)} %stack.2), calls=%async_computation | async-start | bytes 2097152 | tf_op jit(solution)/shard_map/all_to_all | solution.py:68
  22.5 180.7 %all-gather.13.cloned.1.call-start = ((), (), s32[]{:S(2)}) async-start(), calls=%async_computation.4 | async-start | bytes 1081344 | tf_op jit(solution)/shard_map/all_gather | solution.py:73
  23.3 381.4 %all-gather.17.cloned.1.call-start = ((), (), s32[]{:S(2)}) async-start(), calls=%async_computation.7 | async-start | bytes 17301504 | tf_op jit(solution)/shard_map/all_gather | solution.py:30
  24.0 33.0 %copy-start.11 = (f32[512]{0:T(512)}, f32[512]{0:T(512)S(1)}, u32[]{:S(2)}) copy-start(f32[512]{0:T(512)S(1)} %subtract_abs_fusion) | copy-start | bytes 6148
  38.3 18.7 %copy-start.14 = (f32[2]{0:T(128)}, f32[2]{0:T(128)S(1)}, u32[]{:S(2)}) copy-start(f32[2]{0:T(128)S(1)} %power_multiply_fusion) | copy-start | bytes 28
  38.3 207.4 %copy-start.13 = (f32[2,512]{1,0:T(2,128)}, f32[2,512]{1,0:T(2,128)S(1)}, u32[]{:S(2)}) copy-start(f32[2,512]{1,0:T(2,128)S(1)} %broadcast_multiply_fusion.1) | copy-start | bytes 12292
  208.0 39.7 %copy-start.8 = (bf16[1024,256]{0,1:T(8,128)(2,1)S(1)}, bf16[1024,256]{0,1:T(8,128)(2,1)}, u32[]{:S(2)}) copy-start(bf16[1024,256]{0,1:T(8,128)(2,1)} %copy.45) | copy-start | bytes 1572868
  245.8 2.0 copy-start
  249.8 321.9 %all-gather.15.cloned.1.call-start = ((), (), s32[]{:S(2)}) async-start(), calls=%async_computation.5 | async-start | bytes 1081344 | tf_op jit(solution)/shard_map/all_gather | solution.py:184
  250.4 361.1 %reduce-scatter.2.cloned.1.call-start = ((), (), s32[]{:S(2)}) async-start(), calls=%async_computation.6 | async-start | bytes 4792320 | tf_op jit(solution)/shard_map/reduce_scatter | solution.py:187
  250.5 81.0 %collective-permute-start = (bf16[256,512]{1,0:T(8,128)(2,1)S(1)}, bf16[256,512]{1,0:T(8,128)(2,1)S(1)}, u32[]{:S(2)}, u32[]{:S(2)}) collective-permute-start(bf16[256,512]{1,0:T(8,128)(2,1)S(1)} %get-tuple-element.403), channel_id=1, source_target_pairs={{0,8},{8,16},{16,24},{24,32},{32,40},{40,48},{48,56},{56,64},{64,7... | collective-permute-start | bytes 786440 | tf_op jit(solution)/shard_map/ppermute | solution.py:23
  252.9 79.2 %collective-permute-start.1 = (bf16[256,512]{1,0:T(8,128)(2,1)S(1)}, bf16[256,512]{1,0:T(8,128)(2,1)}, u32[]{:S(2)}, u32[]{:S(2)}) collective-permute-start(bf16[256,512]{1,0:T(8,128)(2,1)S(1)} %get-tuple-element.404), channel_id=1, source_target_pairs={{8,0},{16,8},{24,16},{32,24},{40,32},{48,40},{56,48},{64,56},{72,6... | collective-permute-start | bytes 786440 | tf_op jit(solution)/shard_map/ppermute | solution.py:24
  331.5 0.6 copy-start.10
  333.7 2.9 copy-start.3
  341.5 1.3 copy-start.1
  341.5 2.1 copy-start.9
  342.7 1.5 copy-start.5
  342.7 2.3 copy-start.4
  344.2 0.8 copy-start.6
  345.1 2.9 copy-start.3
  352.8 1.3 copy-start.1
  352.8 2.1 copy-start.9
  354.1 1.5 copy-start.5
  354.1 2.3 copy-start.4
  355.6 0.8 copy-start.6
  430.9 140.7 %copy-start.7 = (bf16[2,512,256]{2,1,0:T(8,128)(2,1)S(1)}, bf16[2,512,256]{2,1,0:T(8,128)(2,1)}, u32[]{:S(2)}) copy-start(bf16[2,512,256]{2,1,0:T(8,128)(2,1)} %get-tuple-element.294) | copy-start | bytes 1572868
  576.2 0.7 copy-start.15
  576.2 35.3 %copy-start.2 = (bf16[1024,256]{1,0:T(8,128)(2,1)S(1)}, bf16[1024,256]{1,0:T(8,128)(2,1)}, u32[]{:S(2)}) copy-start(bf16[1024,256]{1,0:T(8,128)(2,1)} %param.13) | copy-start | bytes 1572868
  576.2 35.3 %copy-start.12 = (bf16[16,256]{1,0:T(8,128)(2,1)S(1)}, bf16[16,256]{1,0:T(8,128)(2,1)}, u32[]{:S(2)}) copy-start(bf16[16,256]{1,0:T(8,128)(2,1)} %param.14) | copy-start | bytes 24580
  576.2 52.0 %copy-start.16 = (f32[256]{0:T(256)S(1)}, f32[256]{0:T(256)}, u32[]{:S(2)}) copy-start(f32[256]{0:T(256)} %param.19) | copy-start | bytes 3076
Sparse Core Ops, SparseCore 0:
  9.8 42.4 all-gather.8
  54.8 71.8 all-gather.10
  129.3 73.8 all-gather.12
  249.9 154.7 all-gather.16
  407.1 68.5 all-gather.14
  576.4 35.1 reduce-scatter.1
